TPU v7x, 1024 devices: a whole 4x4x32 slice. The times are simulated.
1024 devices in a mesh: grp: 64 (over y, x, z_hi), mem: 16 (over z_lo, core).
Axes of the slice: x: 4, y: 4, z: 32 (z_hi: 4, z_lo: 8; z = z_hi * 8 + z_lo), core: 2. Of those that a mesh axis runs over, the one named last changes fastest.
Arguments:
- stem: bfloat16 [2, 64, 16, 1024, 256], P(None, 'grp', 'mem'), may hold values from -6 to 6
- branches: bfloat16 [3, 2, 256, 256], replicated, may hold values from -0.25 to 0.25
- mode_order: int32 [3, 256], replicated, may hold values from 0 to 255, each once within a row
Outputs:
- contracted: bfloat16 [2, 64, 16, 1024, 256], P(None, 'grp', 'mem')
Inputs may be any that keep to these rules, and one draw needn't show every extreme that they name: Each row of mode_order names every number below 256 once.
All inputs are finite; a program needn't handle non-finite values.
Results may differ from a plain program's by a relative error of at most 0.0057.
Values may be sent and summed in bfloat16 or wider, within the bound.
A program may use at most 32 MiB of HBM per device.

v0:
```python
import jax
import jax.numpy as jnp
from jax import lax
from jax.sharding import PartitionSpec as P


def real_matrix(branches, mode_order, section_no):
    weight = jnp.take(branches[section_no], mode_order[section_no], axis=1)
    upper = jnp.concatenate([weight[0], weight[1]], axis=1)
    lower = jnp.concatenate([-weight[1], weight[0]], axis=1)
    return jnp.concatenate([upper, lower], axis=0)


def contract_columns(arrived, real_form):
    row_count = arrived.shape[-1]
    half = real_form.shape[1] // 2
    joined = arrived.reshape(2 * half, row_count)
    result = lax.dot_general(
        real_form, joined, (((0,), (0,)), ((), ())), preferred_element_type=jnp.float32
    )
    return result.astype(jnp.bfloat16).reshape(2, half, row_count)


def local(stem, branches, mode_order):
    forms = [real_matrix(branches, mode_order, section_no) for section_no in range(3)]
    row_count = stem.shape[3]
    width = stem.shape[4]
    inner_count = lax.axis_size("mem")
    outer_count = lax.axis_size("grp")
    local_stem = stem[:, 0, 0]
    joined = jnp.concatenate([local_stem[0], local_stem[1]], axis=-1)
    first_full = lax.dot_general(
        forms[0], joined, (((0,), (1,)), ((), ())), preferred_element_type=jnp.float32
    )
    first = first_full.astype(jnp.bfloat16).reshape(2, width, row_count)
    inner_pieces = first.reshape(2, inner_count, width // inner_count, row_count)
    arrived_inner = lax.all_to_all(inner_pieces, "mem", split_axis=1, concat_axis=1, tiled=True)
    second = contract_columns(arrived_inner, forms[1])
    outer_pieces = second.reshape(2, outer_count, width // outer_count, row_count)
    arrived_outer = lax.all_to_all(outer_pieces, "grp", split_axis=1, concat_axis=1, tiled=True)
    final = contract_columns(arrived_outer, forms[2])
    return jnp.transpose(final, (0, 2, 1)).reshape(2, 1, 1, row_count, width)


def solution(mesh):
    in_specs = (P(None, "grp", "mem", None, None), P(), P())
    out_specs = P(None, "grp", "mem", None, None)
    return jax.shard_map(local, mesh=mesh, in_specs=in_specs, out_specs=out_specs, check_vma=False)
```

profile of v0, /device:TPU:192, one launch (start us, length us, event | category | flops | bytes accessed | tf_op | source)
XLA Modules:
  0.0 207.0 jit_solution(1620738655963304929)
XLA Ops:
  0.0 0.8 fusion.37
  0.8 1.2 fusion.33
  2.0 0.5 copy_bitcast_fusion
  2.5 1.2 gather_fusion.2
  3.8 0.9 fusion.26
  4.7 0.0 copy-start
  4.8 0.4 fusion.36
  5.2 0.8 copy-done
  6.0 0.1 slice_bitcast_fusion.1
  6.0 0.8 convolution_convert_fusion.2
  6.8 1.0 copy.29
  7.9 14.0 %all-to-all-start = ((bf16[2,16,16,1024]{3,2,0,1:T(8,128)(2,1)}), bf16[2,16,16,1024]{3,2,0,1:T(8,128)(2,1)S(1)}, u32[]{:S(2)}, u32[]{:S(2)}) async-start(bf16[2,16,16,1024]{3,2,0,1:T(8,128)(2,1)} %copy.29), calls=%async_computation | async-start | bytes 2097152 | tf_op jit(solution)/shard_map/all_to_all | solution.py:37
  21.9 1.2 gather_fusion.1
  23.1 0.9 fusion.25
  24.1 0.4 fusion.35
  24.5 41.3 %all-to-all-done = bf16[2,16,16,1024]{3,2,0,1:T(8,128)(2,1)S(1)} async-done(((bf16[2,16,16,1024]{3,2,0,1:T(8,128)(2,1)}), bf16[2,16,16,1024]{3,2,0,1:T(8,128)(2,1)S(1)}, u32[]{:S(2)}, u32[]{:S(2)}) %all-to-all-start) | async-done | bytes 1048608 | tf_op jit(solution)/shard_map/all_to_all | solution.py:37
  65.8 0.1 copy.30
  65.9 0.7 convolution_convert_fusion.1
  66.6 0.4 reshape_reshape.7
  67.1 1.6 copy.31
  68.6 23.4 %all-to-all-start.1 = ((bf16[2,64,4,1024]{3,2,0,1:T(4,128)(2,1)}), bf16[2,64,4,1024]{3,2,0,1:T(4,128)(2,1)S(1)}, u32[]{:S(2)}, u32[]{:S(2)}) async-start(bf16[2,64,4,1024]{3,2,0,1:T(4,128)(2,1)} %copy.31), calls=%async_computation.1 | async-start | bytes 2097152 | tf_op jit(solution)/shard_map/all_to_all | solution.py:40
  92.0 0.3 copy.55
  92.3 1.2 gather_fusion
  93.6 0.9 fusion.24
  94.5 0.4 fusion.34
  95.0 109.3 %all-to-all-done.1 = bf16[2,64,4,1024]{3,2,0,1:T(4,128)(2,1)S(1)} async-done(((bf16[2,64,4,1024]{3,2,0,1:T(4,128)(2,1)}), bf16[2,64,4,1024]{3,2,0,1:T(4,128)(2,1)S(1)}, u32[]{:S(2)}, u32[]{:S(2)}) %all-to-all-start.1) | async-done | bytes 1048608 | tf_op jit(solution)/shard_map/all_to_all | solution.py:40
  204.3 0.4 copy.32
  204.6 0.3 reshape.22
  204.9 0.7 convolution_convert_fusion
  205.6 1.3 copy.33
  (15 shorter events, 0.2 us)
Async XLA Ops:
  4.7 1.2 copy-start
  7.9 57.9 %all-to-all-start = ((bf16[2,16,16,1024]{3,2,0,1:T(8,128)(2,1)}), bf16[2,16,16,1024]{3,2,0,1:T(8,128)(2,1)S(1)}, u32[]{:S(2)}, u32[]{:S(2)}) async-start(bf16[2,16,16,1024]{3,2,0,1:T(8,128)(2,1)} %copy.29), calls=%async_computation | async-start | bytes 2097152 | tf_op jit(solution)/shard_map/all_to_all | solution.py:37
  68.6 135.6 %all-to-all-start.1 = ((bf16[2,64,4,1024]{3,2,0,1:T(4,128)(2,1)}), bf16[2,64,4,1024]{3,2,0,1:T(4,128)(2,1)S(1)}, u32[]{:S(2)}, u32[]{:S(2)}) async-start(bf16[2,64,4,1024]{3,2,0,1:T(4,128)(2,1)} %copy.31), calls=%async_computation.1 | async-start | bytes 2097152 | tf_op jit(solution)/shard_map/all_to_all | solution.py:40
where the time goes:
time: 207 us
  waiting for transfers between devices  151 us (73%)
  starting transfers between devices  37.4 us (18%)
  local copies, waits for them, and re-layouts  13.6 us (7%)
  other arithmetic  2.97 us (1%)
  matrix products  2.23 us (1%)
    all_to_all x1, waiting for transfers between devices, local(): lax.all_to_all(outer_pieces, 'grp', split_axis=1, concat_axis=1, tiled=True)  109 us
    all_to_all x1, waiting for transfers between devices, local(): lax.all_to_all(inner_pieces, 'mem', split_axis=1, concat_axis=1, tiled=True)  41.3 us
    all_to_all x1, starting transfers between devices, local(): lax.all_to_all(outer_pieces, 'grp', split_axis=1, concat_axis=1, tiled=True)  23.4 us
    all_to_all x1, starting transfers between devices, local(): lax.all_to_all(inner_pieces, 'mem', split_axis=1, concat_axis=1, tiled=True)  14 us
  transfers between devices with their start and end apart: 2, of which 2 were waited for; matrix products, arithmetic and copies ran while one was open for 3% of the time, Pallas kernels for 0%

commit v1 on v0

v1 whole, which is shorter than its diff:
```python
import functools

import jax
import jax.numpy as jnp
from jax import lax
from jax.experimental import pallas as pl
from jax.experimental.pallas import tpu as pltpu
from jax.sharding import PartitionSpec as P

MESH = pl.DeviceIdType.MESH
CHUNKS = 4
NX = 4
NZ = 4


def dot(a, b, contract):
    return lax.dot_general(a, b, ((contract[:1], contract[1:]), ((), ())), preferred_element_type=jnp.float32)


def one_hot(shape, dim, of_other):
    mine = lax.broadcasted_iota(jnp.int32, shape, dim)
    other = lax.broadcasted_iota(jnp.int32, shape, 1 - dim)
    return jnp.where(mine == of_other(other), 1.0, 0.0).astype(jnp.bfloat16)


def kernel(geom, stem_ref, branch_ref, mode_ref, out_ref, w0, w1, w2, first, arr1, sec, xarr, relp, relm, zarr,
           s1, r1, sx, rx, sz, rz, own_sem):
    nm, nxy, nx, nz, chunks = geom
    ny = nxy // nx
    block = stem_ref.shape[2]
    rows = stem_ref.shape[1] // chunks
    u2, u3 = block // nm, block // (nxy * nz)
    half = nxy // 2
    me = lax.axis_index("mem")
    grp = lax.axis_index("grp")
    zh, xy = lax.rem(grp, nz), lax.div(grp, nz)
    yi, xi = lax.div(xy, nx), lax.rem(xy, nx)
    zp, zm, z2 = lax.rem(zh + 1, nz), lax.rem(zh + nz - 1, nz), lax.rem(zh + 2, nz)
    plus, minus = {"grp": xy * nz + zp}, {"grp": xy * nz + zm}

    mem_peers = [lax.rem(me + d, nm) for d in range(1, nm)]
    xy_peers = []
    for d in range(1, nxy):
        dy, dx = d // nx, d % nx
        xy_peers.append(lax.rem(yi + dy, ny) * nx + lax.rem(xi + dx, nx))

    barrier = pltpu.get_barrier_semaphore()
    for peer in mem_peers:
        pl.semaphore_signal(barrier, inc=1, device_id={"mem": peer}, device_id_type=MESH)
    for peer in xy_peers:
        pl.semaphore_signal(barrier, inc=1, device_id={"grp": peer * nz + zh}, device_id_type=MESH)
    for target in (plus, minus):
        pl.semaphore_signal(barrier, inc=1, device_id=target, device_id_type=MESH)

    def natural(k):
        order = mode_ref[pl.ds(k, 1), :]
        hot = jnp.where(lax.broadcasted_iota(jnp.int32, (block, block), 0) == order, 1.0, 0.0).astype(jnp.bfloat16)
        re = dot(branch_ref[k, 0], hot, (0, 0)).astype(jnp.bfloat16)
        im = dot(branch_ref[k, 1], hot, (0, 0)).astype(jnp.bfloat16)
        top = jnp.concatenate([re, -im], axis=1)
        bottom = jnp.concatenate([im, re], axis=1)
        return jnp.concatenate([top, bottom], axis=0)

    full = (2 * block, 2 * block)

    def by_unit(unit):
        def place(p):
            u, c, l = lax.div(p, 2 * unit), lax.rem(lax.div(p, unit), 2), lax.rem(p, unit)
            return c * block + u * unit + l
        return place

    def by_arrival(p):
        l, c = lax.rem(p, u3), lax.rem(lax.div(p, u3), 2)
        src = lax.rem(lax.div(p, 2 * u3), nxy)
        z = lax.div(p, 2 * u3 * nxy)
        return c * block + (src * nz + z) * u3 + l

    w0[...] = dot(one_hot(full, 1, by_unit(u2)), natural(0), (1, 0)).astype(jnp.bfloat16)

    pl.semaphore_wait(barrier, (nm - 1) + (nxy - 1) + 2)

    def remote(src, dst, send, recv, target):
        return pltpu.make_async_remote_copy(src_ref=src, dst_ref=dst, send_sem=send, recv_sem=recv,
                                            device_id=target, device_id_type=MESH)

    def copies_one(c):
        return [remote(first.at[c, peer], arr1.at[c, me], s1.at[c, d], r1.at[c, d], {"mem": peer})
                for d, peer in enumerate(mem_peers)]

    def arrivals_one(c):
        for d in range(nm - 1):
            src = lax.rem(me + nm - (d + 1), nm)
            remote(first.at[c, src], arr1.at[c, src], s1.at[c, d], r1.at[c, d], {"mem": src}).wait_recv()

    def own_one(c):
        return pltpu.make_async_copy(first.at[c, me], arr1.at[c, me], own_sem.at[c, 0])

    def copies_xy(c):
        return [remote(sec.at[c, peer], xarr.at[c, :, xy], sx.at[c, d], rx.at[c, d], {"grp": peer * nz + zh})
                for d, peer in enumerate(xy_peers)]

    def arrivals_xy(c):
        for d in range(nxy - 1):
            dy, dx = (d + 1) // nx, (d + 1) % nx
            src = lax.rem(yi + ny - dy, ny) * nx + lax.rem(xi + nx - dx, nx)
            remote(sec.at[c, src], xarr.at[c, :, src], sx.at[c, d], rx.at[c, d], {"grp": src * nz + zh}).wait_recv()

    def own_xy(c):
        return pltpu.make_async_copy(sec.at[c, xy], xarr.at[c, :, xy], own_sem.at[c, 1])

    low, high = pl.ds(0, half), pl.ds(half, nxy - half)

    def copies_z(c):
        return [
            remote(xarr.at[c, z2, low], relp.at[c], sz.at[c, 0], rz.at[c, 0], plus),
            remote(xarr.at[c, z2, high], relm.at[c], sz.at[c, 1], rz.at[c, 1], minus),
            remote(xarr.at[c, zp], zarr.at[c, zh], sz.at[c, 2], rz.at[c, 2], plus),
            remote(xarr.at[c, zm], zarr.at[c, zh], sz.at[c, 3], rz.at[c, 3], minus),
        ]

    def own_z(c):
        return pltpu.make_async_copy(xarr.at[c, zh], zarr.at[c, zh], own_sem.at[c, 2])

    def copies_on(c):
        return [
            remote(relp.at[c], zarr.at[c, zm, low], sz.at[c, 4], rz.at[c, 4], plus),
            remote(relm.at[c], zarr.at[c, zp, high], sz.at[c, 5], rz.at[c, 5], minus),
        ]

    def arrivals_z(c):
        remote(xarr.at[c, zm], zarr.at[c, zm], sz.at[c, 2], rz.at[c, 2], plus).wait_recv()
        remote(xarr.at[c, zp], zarr.at[c, zp], sz.at[c, 3], rz.at[c, 3], minus).wait_recv()
        remote(relp.at[c], zarr.at[c, z2, low], sz.at[c, 4], rz.at[c, 4], plus).wait_recv()
        remote(relm.at[c], zarr.at[c, z2, high], sz.at[c, 5], rz.at[c, 5], minus).wait_recv()

    def stage_one(c):
        here = pl.ds(c * rows, rows)
        out = dot(w0[:, :block], stem_ref[0, here, :], (1, 1)) + dot(w0[:, block:], stem_ref[1, here, :], (1, 1))
        first[c] = out.astype(jnp.bfloat16).reshape(nm, 2 * u2, rows)
        own_one(c).start()
        for copy in copies_one(c):
            copy.start()

    def stage_two(c):
        own_one(c).wait()
        arrivals_one(c)
        out = dot(w1[...], arr1[c].reshape(2 * block, rows), (1, 0))
        sec[c] = out.astype(jnp.bfloat16).reshape(nxy, nz, 2 * u3, rows)
        own_xy(c).start()
        for copy in copies_xy(c):
            copy.start()

    def stage_z(c):
        own_xy(c).wait()
        arrivals_xy(c)
        for copy in copies_z(c):
            copy.start()
        own_z(c).start()

    def stage_on(c):
        for copy, (buf, i, target) in zip(copies_on(c), ((relp, 0, plus), (relm, 1, minus))):
            remote(buf.at[c], buf.at[c], sz.at[c, i], rz.at[c, i], target).wait_recv()
            copy.start()

    def stage_out(c):
        own_z(c).wait()
        arrivals_z(c)
        out = dot(w2[...], zarr[c].reshape(2 * block, rows), (1, 0))
        turned = jnp.transpose(out).astype(jnp.bfloat16)
        here = pl.ds(c * rows, rows)
        out_ref[0, here, :] = turned[:, :block]
        out_ref[1, here, :] = turned[:, block:]

    for c in range(chunks):
        stage_one(c)
    tmp = dot(one_hot(full, 1, by_unit(u3)), natural(1), (1, 0)).astype(jnp.bfloat16)
    w1[...] = dot(tmp, one_hot(full, 0, by_unit(u2)), (1, 0)).astype(jnp.bfloat16)
    w2[...] = dot(natural(2), one_hot(full, 0, by_arrival), (1, 0)).astype(jnp.bfloat16)
    stages = (stage_two, stage_z, stage_on, stage_out)
    for step in range(chunks + len(stages) - 1):
        for lag, stage in enumerate(stages):
            if 0 <= step - lag < chunks:
                stage(step - lag)
    for c in range(chunks):
        for copy in copies_one(c) + copies_xy(c) + copies_z(c) + copies_on(c):
            copy.wait_send()


def build(geom):
    nm, nxy, nx, nz, chunks = geom

    def local(stem, branches, mode_order):
        stem = stem[:, 0, 0]
        _, row_count, block = stem.shape
        rows = row_count // chunks
        u2, u3 = block // nm, block // (nxy * nz)
        vmem = pl.BlockSpec(memory_space=pltpu.VMEM)
        weight = pltpu.VMEM((2 * block, 2 * block), jnp.bfloat16)
        relay = pltpu.VMEM((chunks, nxy // 2, 2 * u3, rows), jnp.bfloat16)
        out = pl.pallas_call(
            functools.partial(kernel, geom),
            out_shape=jax.ShapeDtypeStruct(stem.shape, jnp.bfloat16),
            in_specs=[vmem] * 3,
            out_specs=vmem,
            scratch_shapes=[
                weight, weight, weight,
                pltpu.VMEM((chunks, nm, 2 * u2, rows), jnp.bfloat16),
                pltpu.VMEM((chunks, nm, 2 * u2, rows), jnp.bfloat16),
                pltpu.VMEM((chunks, nxy, nz, 2 * u3, rows), jnp.bfloat16),
                pltpu.VMEM((chunks, nz, nxy, 2 * u3, rows), jnp.bfloat16),
                relay, relay,
                pltpu.VMEM((chunks, nz, nxy, 2 * u3, rows), jnp.bfloat16),
                pltpu.SemaphoreType.DMA((chunks, nm - 1)),
                pltpu.SemaphoreType.DMA((chunks, nm - 1)),
                pltpu.SemaphoreType.DMA((chunks, nxy - 1)),
                pltpu.SemaphoreType.DMA((chunks, nxy - 1)),
                pltpu.SemaphoreType.DMA((chunks, 6)),
                pltpu.SemaphoreType.DMA((chunks, 6)),
                pltpu.SemaphoreType.DMA((chunks, 3)),
            ],
            compiler_params=pltpu.CompilerParams(
                collective_id=0, has_side_effects=True, vmem_limit_bytes=48 << 20
            ),
        )(stem, branches, mode_order)
        return out.reshape(2, 1, 1, row_count, block)

    return local


def solution(mesh):
    geom = (mesh.shape["mem"], mesh.shape["grp"] // NZ, NX, NZ, CHUNKS)
    in_specs = (P(None, "grp", "mem", None, None), P(), P())
    out_specs = P(None, "grp", "mem", None, None)
    return jax.shard_map(build(geom), mesh=mesh, in_specs=in_specs, out_specs=out_specs, check_vma=False)
```

time: 207 us -> 176 us (0.85)
  the two profiles are of different devices: /device:TPU:192 before, /device:TPU:96 now
where the time goes in v1:
time: 176 us
  Pallas kernels  172 us (98%)
  local copies, waits for them, and re-layouts  4.02 us (2%)
    pallas_call x1, Pallas kernels, local(): pl.pallas_call(functools.partial(kernel, geom), out_shape=jax.ShapeDtypeS...  172 us
    unnamed x7, local copies, waits for them, and re-layouts  4.02 us

profile of v1, /device:TPU:96, one launch (start us, length us, event | category | flops | bytes accessed | tf_op | source)
XLA Modules:
  0.0 175.8 jit_solution(13828472734576990913)
XLA Ops:
  0.0 0.0 copy-start
  0.0 1.2 copy-done
  1.2 0.0 copy-start.1
  1.2 1.1 copy-done.1
  2.4 0.0 copy-start.2
  2.4 0.7 copy-done.2
  3.0 171.8 %shard_map.37 = bf16[2,1024,256]{2,1,0:T(8,128)(2,1)S(1)} custom-call(bf16[2,1024,256]{2,1,0:T(8,128)(2,1)S(1)} %bitcast.5, bf16[3,2,256,256]{3,2,1,0:T(8,128)(2,1)S(1)} %copy-done.1, s32[3,256]{1,0:T(4,128)S(1)} %copy-done.2), custom_call_target="tpu_custom_call" | custom-call | tf_op jit(solution)/shard_map/pallas_call | solution.py:200
  174.8 1.0 copy.6
Async XLA Ops:
  0.0 1.2 copy-start
  1.2 1.1 copy-start.1
  2.4 0.7 copy-start.2

commit v2 on v1

--- a/solution.py
+++ b/solution.py
@@ -8,7 +8,14 @@
 from jax.sharding import PartitionSpec as P
 
 MESH = pl.DeviceIdType.MESH
-CHUNKS = 4
+CHUNKS = 2
+Z_LAG = 1
+
+
+def MEM_ORDER(nm):
+    return list(range(nm // 2, nm)) + list(range(1, nm // 2))
+
+
 NX = 4
 NZ = 4
 
@@ -19,12 +26,13 @@
 
 def one_hot(shape, dim, of_other):
     mine = lax.broadcasted_iota(jnp.int32, shape, dim)
-    other = lax.broadcasted_iota(jnp.int32, shape, 1 - dim)
-    return jnp.where(mine == of_other(other), 1.0, 0.0).astype(jnp.bfloat16)
-
-
-def kernel(geom, stem_ref, branch_ref, mode_ref, out_ref, w0, w1, w2, first, arr1, sec, xarr, relp, relm, zarr,
-           s1, r1, sx, rx, sz, rz, own_sem):
+    line = (shape[0], 1) if dim == 1 else (1, shape[1])
+    other = of_other(lax.broadcasted_iota(jnp.int32, line, 1 - dim))
+    return jnp.where(mine == other, 1.0, 0.0).astype(jnp.bfloat16)
+
+
+def kernel(geom, stem_hbm, branch_hbm, mode_hbm, out_ref, stem_ref, branch_ref, mode_ref, w0, w1, w2, first, arr1, sec, xarr, relp, relm, zarr,
+           s1, r1, sx, rx, sz, rz, own_sem, in_sem):
     nm, nxy, nx, nz, chunks = geom
     ny = nxy // nx
     block = stem_ref.shape[2]
@@ -38,7 +46,11 @@
     zp, zm, z2 = lax.rem(zh + 1, nz), lax.rem(zh + nz - 1, nz), lax.rem(zh + 2, nz)
     plus, minus = {"grp": xy * nz + zp}, {"grp": xy * nz + zm}
 
-    mem_peers = [lax.rem(me + d, nm) for d in range(1, nm)]
+    def flipped(d):
+        bits = [1 << b for b in range(nm.bit_length() - 1) if d & (1 << b)]
+        return me + sum(bit * (1 - 2 * lax.rem(lax.div(me, bit), 2)) for bit in bits)
+
+    mem_peers = [flipped(d) for d in MEM_ORDER(nm)]
     xy_peers = []
     for d in range(1, nxy):
         dy, dx = d // nx, d % nx
@@ -52,11 +64,27 @@
     for target in (plus, minus):
         pl.semaphore_signal(barrier, inc=1, device_id=target, device_id_type=MESH)
 
-    def natural(k):
+    fetch_mode = pltpu.make_async_copy(mode_hbm, mode_ref, in_sem.at[0])
+    fetch_branch = [pltpu.make_async_copy(branch_hbm.at[k], branch_ref.at[k], in_sem.at[1 + k]) for k in range(3)]
+    fetch_stem = [pltpu.make_async_copy(stem_hbm.at[:, pl.ds(c * rows, rows)], stem_ref.at[:, pl.ds(c * rows, rows)],
+                                        in_sem.at[4 + c]) for c in range(chunks)]
+    fetch_mode.start()
+    fetch_branch[0].start()
+    for fetch in fetch_stem:
+        fetch.start()
+    fetch_branch[1].start()
+    fetch_branch[2].start()
+
+    def parts(k):
+        fetch_branch[k].wait()
         order = mode_ref[pl.ds(k, 1), :]
         hot = jnp.where(lax.broadcasted_iota(jnp.int32, (block, block), 0) == order, 1.0, 0.0).astype(jnp.bfloat16)
         re = dot(branch_ref[k, 0], hot, (0, 0)).astype(jnp.bfloat16)
         im = dot(branch_ref[k, 1], hot, (0, 0)).astype(jnp.bfloat16)
+        return re, im
+
+    def natural(k):
+        re, im = parts(k)
         top = jnp.concatenate([re, -im], axis=1)
         bottom = jnp.concatenate([im, re], axis=1)
         return jnp.concatenate([top, bottom], axis=0)
@@ -75,7 +103,12 @@
         z = lax.div(p, 2 * u3 * nxy)
         return c * block + (src * nz + z) * u3 + l
 
-    w0[...] = dot(one_hot(full, 1, by_unit(u2)), natural(0), (1, 0)).astype(jnp.bfloat16)
+    fetch_mode.wait()
+    re, im = (part.reshape(nm, u2, block) for part in parts(0))
+    w0[:, 0, :, :block] = re
+    w0[:, 0, :, block:] = -im
+    w0[:, 1, :, :block] = im
+    w0[:, 1, :, block:] = re
 
     pl.semaphore_wait(barrier, (nm - 1) + (nxy - 1) + 2)
 
@@ -88,8 +121,7 @@
                 for d, peer in enumerate(mem_peers)]
 
     def arrivals_one(c):
-        for d in range(nm - 1):
-            src = lax.rem(me + nm - (d + 1), nm)
+        for d, src in enumerate(mem_peers):
             remote(first.at[c, src], arr1.at[c, src], s1.at[c, d], r1.at[c, d], {"mem": src}).wait_recv()
 
     def own_one(c):
@@ -135,7 +167,9 @@
 
     def stage_one(c):
         here = pl.ds(c * rows, rows)
-        out = dot(w0[:, :block], stem_ref[0, here, :], (1, 1)) + dot(w0[:, block:], stem_ref[1, here, :], (1, 1))
+        fetch_stem[c].wait()
+        form = w0[...].reshape(full)
+        out = dot(form[:, :block], stem_ref[0, here, :], (1, 1)) + dot(form[:, block:], stem_ref[1, here, :], (1, 1))
         first[c] = out.astype(jnp.bfloat16).reshape(nm, 2 * u2, rows)
         own_one(c).start()
         for copy in copies_one(c):
@@ -166,7 +200,7 @@
         own_z(c).wait()
         arrivals_z(c)
         out = dot(w2[...], zarr[c].reshape(2 * block, rows), (1, 0))
-        turned = jnp.transpose(out).astype(jnp.bfloat16)
+        turned = jnp.transpose(out.astype(jnp.bfloat16))
         here = pl.ds(c * rows, rows)
         out_ref[0, here, :] = turned[:, :block]
         out_ref[1, here, :] = turned[:, block:]
@@ -176,11 +210,18 @@
     tmp = dot(one_hot(full, 1, by_unit(u3)), natural(1), (1, 0)).astype(jnp.bfloat16)
     w1[...] = dot(tmp, one_hot(full, 0, by_unit(u2)), (1, 0)).astype(jnp.bfloat16)
     w2[...] = dot(natural(2), one_hot(full, 0, by_arrival), (1, 0)).astype(jnp.bfloat16)
-    stages = (stage_two, stage_z, stage_on, stage_out)
-    for step in range(chunks + len(stages) - 1):
-        for lag, stage in enumerate(stages):
-            if 0 <= step - lag < chunks:
-                stage(step - lag)
+    done = 0
+    for step in range(chunks):
+        stage_two(step)
+        while done <= step - Z_LAG:
+            stage_z(done)
+            done += 1
+    for c in range(done, chunks):
+        stage_z(c)
+    for c in range(chunks):
+        stage_on(c)
+    for c in range(chunks):
+        stage_out(c)
     for c in range(chunks):
         for copy in copies_one(c) + copies_xy(c) + copies_z(c) + copies_on(c):
             copy.wait_send()
@@ -200,10 +241,14 @@
         out = pl.pallas_call(
             functools.partial(kernel, geom),
             out_shape=jax.ShapeDtypeStruct(stem.shape, jnp.bfloat16),
-            in_specs=[vmem] * 3,
+            in_specs=[pl.BlockSpec(memory_space=pl.ANY)] * 3,
             out_specs=vmem,
             scratch_shapes=[
-                weight, weight, weight,
+                pltpu.VMEM(stem.shape, jnp.bfloat16),
+                pltpu.VMEM(branches.shape, jnp.bfloat16),
+                pltpu.VMEM(mode_order.shape, jnp.int32),
+                pltpu.VMEM((nm, 2, u2, 2 * block), jnp.bfloat16),
+                weight, weight,
                 pltpu.VMEM((chunks, nm, 2 * u2, rows), jnp.bfloat16),
                 pltpu.VMEM((chunks, nm, 2 * u2, rows), jnp.bfloat16),
                 pltpu.VMEM((chunks, nxy, nz, 2 * u3, rows), jnp.bfloat16),
@@ -217,9 +262,10 @@
                 pltpu.SemaphoreType.DMA((chunks, 6)),
                 pltpu.SemaphoreType.DMA((chunks, 6)),
                 pltpu.SemaphoreType.DMA((chunks, 3)),
+                pltpu.SemaphoreType.DMA((4 + chunks,)),
             ],
             compiler_params=pltpu.CompilerParams(
-                collective_id=0, has_side_effects=True, vmem_limit_bytes=48 << 20
+                collective_id=0, has_side_effects=True
             ),
         )(stem, branches, mode_order)
         return out.reshape(2, 1, 1, row_count, block)

time: 176 us -> 171 us (0.972)
  the two profiles are of different devices: /device:TPU:96 before, /device:TPU:201 now
where the time goes in v2:
time: 171 us
  Pallas kernels  168 us (98%)
  local copies, waits for them, and re-layouts  2.26 us (1%)
    pallas_call x1, Pallas kernels, local(): pl.pallas_call(functools.partial(kernel, geom), out_shape=jax.ShapeDtypeS...  168 us

profile of v2, /device:TPU:201, one launch (start us, length us, event | category | flops | bytes accessed | tf_op | source)
XLA Modules:
  0.0 170.6 jit_solution(11218306432522741245)
XLA Ops:
  0.0 168.3 %shard_map.37 = bf16[2,1024,256]{2,1,0:T(8,128)(2,1)} custom-call(bf16[2,1024,256]{2,1,0:T(8,128)(2,1)} %bitcast.5, bf16[3,2,256,256]{3,2,1,0:T(8,128)(2,1)} %branch_hbm.1, s32[3,256]{1,0:T(4,128)} %mode_hbm.1), custom_call_target="tpu_custom_call" | custom-call | tf_op jit(solution)/shard_map/pallas_call | solution.py:241
  168.3 2.3 %copy.6 = bf16[2,1,1,1024,256]{4,3,2,1,0:T(8,128)(2,1)} copy(bf16[2,1,1,1024,256]{4,3,2,1,0:T(8,128)(2,1)} %bitcast.4) | data formatting | bytes 2097152

commit v3 on v2

--- a/solution.py
+++ b/solution.py
@@ -13,7 +13,7 @@
 
 
 def MEM_ORDER(nm):
-    return list(range(nm // 2, nm)) + list(range(1, nm // 2))
+    return list(range(nm // 2, nm)) + list(range(nm // 4, nm // 2)) + list(range(1, nm // 4))
 
 
 NX = 4
@@ -110,8 +110,6 @@
     w0[:, 1, :, :block] = im
     w0[:, 1, :, block:] = re
 
-    pl.semaphore_wait(barrier, (nm - 1) + (nxy - 1) + 2)
-
     def remote(src, dst, send, recv, target):
         return pltpu.make_async_remote_copy(src_ref=src, dst_ref=dst, send_sem=send, recv_sem=recv,
                                             device_id=target, device_id_type=MESH)
@@ -171,9 +169,11 @@
         form = w0[...].reshape(full)
         out = dot(form[:, :block], stem_ref[0, here, :], (1, 1)) + dot(form[:, block:], stem_ref[1, here, :], (1, 1))
         first[c] = out.astype(jnp.bfloat16).reshape(nm, 2 * u2, rows)
-        own_one(c).start()
+
+    def send_one(c):
         for copy in copies_one(c):
             copy.start()
+        own_one(c).start()
 
     def stage_two(c):
         own_one(c).wait()
@@ -187,8 +187,17 @@
     def stage_z(c):
         own_xy(c).wait()
         arrivals_xy(c)
-        for copy in copies_z(c):
-            copy.start()
+        relay_plus, relay_minus, direct_plus, direct_minus = copies_z(c)
+        for early, relay, direct in ((zh == nz - 1, relay_plus, direct_plus), (zh == 1, relay_minus, direct_minus)):
+            @pl.when(early)
+            def _(relay=relay, direct=direct):
+                direct.start()
+                relay.start()
+
+            @pl.when(jnp.logical_not(early))
+            def _(relay=relay, direct=direct):
+                relay.start()
+                direct.start()
         own_z(c).start()
 
     def stage_on(c):
@@ -207,6 +216,9 @@
 
     for c in range(chunks):
         stage_one(c)
+    pl.semaphore_wait(barrier, (nm - 1) + (nxy - 1) + 2)
+    for c in range(chunks):
+        send_one(c)
     tmp = dot(one_hot(full, 1, by_unit(u3)), natural(1), (1, 0)).astype(jnp.bfloat16)
     w1[...] = dot(tmp, one_hot(full, 0, by_unit(u2)), (1, 0)).astype(jnp.bfloat16)
     w2[...] = dot(natural(2), one_hot(full, 0, by_arrival), (1, 0)).astype(jnp.bfloat16)

time: 171 us -> 170 us (level)
  the two profiles are of different devices: /device:TPU:201 before, /device:TPU:65 now
where the time goes in v3:
time: 170 us
  Pallas kernels  168 us (99%)
  local copies, waits for them, and re-layouts  2.26 us (1%)
    pallas_call x1, Pallas kernels, local(): pl.pallas_call(functools.partial(kernel, geom), out_shape=jax.ShapeDtypeS...  168 us

profile of v3, /device:TPU:65, one launch (start us, length us, event | category | flops | bytes accessed | tf_op | source)
XLA Modules:
  0.0 170.1 jit_solution(15520304392918237643)
XLA Ops:
  0.0 167.8 %shard_map.37 = bf16[2,1024,256]{2,1,0:T(8,128)(2,1)} custom-call(bf16[2,1024,256]{2,1,0:T(8,128)(2,1)} %bitcast.5, bf16[3,2,256,256]{3,2,1,0:T(8,128)(2,1)} %branch_hbm.1, s32[3,256]{1,0:T(4,128)} %mode_hbm.1), custom_call_target="tpu_custom_call" | custom-call | tf_op jit(solution)/shard_map/pallas_call | solution.py:253
  167.8 2.3 %copy.6 = bf16[2,1,1,1024,256]{4,3,2,1,0:T(8,128)(2,1)} copy(bf16[2,1,1,1024,256]{4,3,2,1,0:T(8,128)(2,1)} %bitcast.4) | data formatting | bytes 2097152

commit v4 on v3

--- a/solution.py
+++ b/solution.py
@@ -57,12 +57,12 @@
         xy_peers.append(lax.rem(yi + dy, ny) * nx + lax.rem(xi + dx, nx))
 
     barrier = pltpu.get_barrier_semaphore()
+    for target in (plus, minus):
+        pl.semaphore_signal(barrier, inc=1, device_id=target, device_id_type=MESH)
     for peer in mem_peers:
         pl.semaphore_signal(barrier, inc=1, device_id={"mem": peer}, device_id_type=MESH)
     for peer in xy_peers:
         pl.semaphore_signal(barrier, inc=1, device_id={"grp": peer * nz + zh}, device_id_type=MESH)
-    for target in (plus, minus):
-        pl.semaphore_signal(barrier, inc=1, device_id=target, device_id_type=MESH)
 
     fetch_mode = pltpu.make_async_copy(mode_hbm, mode_ref, in_sem.at[0])
     fetch_branch = [pltpu.make_async_copy(branch_hbm.at[k], branch_ref.at[k], in_sem.at[1 + k]) for k in range(3)]

time: 170 us -> 170 us (level)
  no operation moved by 1% of the time
where the time goes in v4:
time: 170 us
  Pallas kernels  168 us (99%)
  local copies, waits for them, and re-layouts  2.26 us (1%)
    pallas_call x1, Pallas kernels, local(): pl.pallas_call(functools.partial(kernel, geom), out_shape=jax.ShapeDtypeS...  168 us

profile of v4, /device:TPU:65, one launch (start us, length us, event | category | flops | bytes accessed | tf_op | source)
XLA Modules:
  0.0 170.1 jit_solution(12049653292017943996)
XLA Ops:
  0.0 167.8 %shard_map.37 = bf16[2,1024,256]{2,1,0:T(8,128)(2,1)} custom-call(bf16[2,1024,256]{2,1,0:T(8,128)(2,1)} %bitcast.5, bf16[3,2,256,256]{3,2,1,0:T(8,128)(2,1)} %branch_hbm.1, s32[3,256]{1,0:T(4,128)} %mode_hbm.1), custom_call_target="tpu_custom_call" | custom-call | tf_op jit(solution)/shard_map/pallas_call | solution.py:253
  167.9 2.3 %copy.6 = bf16[2,1,1,1024,256]{4,3,2,1,0:T(8,128)(2,1)} copy(bf16[2,1,1,1024,256]{4,3,2,1,0:T(8,128)(2,1)} %bitcast.4) | data formatting | bytes 2097152
